TPU v7x, 32 devices: a whole 2x2x4 slice. The times are simulated.
32 devices in a mesh: dp: 16 (over z, y, x), mp: 2 (over core).
Axes of the slice: x: 2, y: 2, z: 4, core: 2. Of those that a mesh axis runs over, the one named last changes fastest.
Arguments:
- tokens: bfloat16 [2, 512, 16, 768], P('mp', 'dp'), may hold values from -6 to 6
- cotangent: bfloat16 [2, 512, 16, 768], P('mp', 'dp'), may hold values from -6 to 6
- lengths: int32 [16], replicated, may hold values from 128 to 1024, as said below
- deal_order: int32 [16], replicated, may hold values from 0 to 15, as said below
- attn_in: bfloat16 [1, 3, 768, 768], P(None, None, 'dp', 'mp'), may hold values from -0.21875 to 0.21875
- attn_out: bfloat16 [1, 768, 768], P(None, 'mp', 'dp'), may hold values from -0.875 to 0.875
- ffn_in: bfloat16 [1, 768, 3072], P(None, 'dp', 'mp'), may hold values from -0.21875 to 0.21875
- ffn_out: bfloat16 [1, 3072, 768], P(None, 'mp', 'dp'), may hold values from -0.109375 to 0.109375
- attn_bias: bfloat16 [1, 2, 768], replicated, may hold values from -3 to 3
- ffn_bias: bfloat16 [1, 3072], replicated, may hold values from -3 to 3
- norm_gain: bfloat16 [1, 2, 768], replicated, may hold values from 0.5 to 1.5
- shifts: bfloat16 [1, 4, 768], replicated, may hold values from -3 to 3
Outputs:
- output: bfloat16 [2, 512, 16, 768], P('mp', 'dp')
- input_grad: bfloat16 [2, 512, 16, 768], P('mp', 'dp')
- attn_in_grad: float32 [1, 3, 768, 768], P(None, None, 'dp', 'mp')
- attn_out_grad: float32 [1, 768, 768], P(None, 'mp', 'dp')
- ffn_in_grad: float32 [1, 768, 3072], P(None, 'dp', 'mp')
- ffn_out_grad: float32 [1, 3072, 768], P(None, 'mp', 'dp')
- attn_bias_grad: float32 [1, 2, 768], replicated
- ffn_bias_grad: float32 [1, 3072], replicated
- norm_gain_grad: float32 [1, 2, 768], replicated
- shifts_grad: float32 [1, 4, 768], replicated
Inputs may be any that keep to these rules, and one draw needn't show every extreme that they name: `lengths`: some sequence has exactly 1024 valid tokens. `deal_order`: a permutation of the sequences; slot s is processed by data group s.
All inputs are finite; a program needn't handle non-finite values.
Results may differ from a plain program's by a relative error of at most 0.02.
Values may be sent and summed in bfloat16 or wider, within the bound.
No kernel may reach another device: no remote copies, remote signals or barrier semaphores. Data moves between devices by JAX's collectives and lax.ppermute only.
A program may use at most 128 MiB of HBM per device.

v0:
```python
import jax
import jax.numpy as jnp
from jax import lax
from jax.sharding import PartitionSpec as P

HEAD_DIM = 64
eps_norm = 1e-12
root_half = 0.7071067811865476
inv_root_two_pi = 0.3989422804014327
negative_fill = -1000000000.0


def gather_rows(rows_low):
    return lax.all_gather(rows_low, "mp", axis=0, tiled=True)


def gather_grads(rows_low):
    return lax.all_gather(rows_low, "mp", axis=0, tiled=True)


def spread_rows(make_term, row_count):
    return lax.psum_scatter(
        make_term(jnp.int32(0), row_count * lax.axis_size("mp")).astype(jnp.bfloat16),
        "mp",
        scatter_dimension=0,
        tiled=True,
    ).astype(jnp.float32)


def spread_grads(make_term, row_count):
    return lax.psum_scatter(
        make_term(jnp.int32(0), row_count * lax.axis_size("mp")).astype(jnp.bfloat16),
        "mp",
        scatter_dimension=0,
        tiled=True,
    ).astype(jnp.float32)


def fetch_weights(three_part, back_part, up_part, down_part):
    return (
        lax.all_gather(three_part, "dp", axis=1, tiled=True),
        lax.all_gather(back_part, "dp", axis=1, tiled=True),
        lax.all_gather(up_part, "dp", axis=0, tiled=True),
        lax.all_gather(down_part, "dp", axis=1, tiled=True),
    )


def fetch_again(three_part, back_part, up_part, down_part):
    return (
        lax.all_gather(three_part, "dp", axis=1, tiled=True),
        lax.all_gather(back_part, "dp", axis=1, tiled=True),
        lax.all_gather(up_part, "dp", axis=0, tiled=True),
        lax.all_gather(down_part, "dp", axis=1, tiled=True),
    )


def contract_rows(left_rows, right_rows):
    return lax.dot_general(
        left_rows, right_rows, (((0,), (0,)), ((), ())), preferred_element_type=jnp.float32
    )


def contract_cols(left_rows, right_rows):
    return lax.dot_general(
        left_rows, right_rows, (((1,), (1,)), ((), ())), preferred_element_type=jnp.float32
    )


def norm_forward(mixed_rows, gain, shift):
    center = mixed_rows - jnp.mean(mixed_rows, axis=1, keepdims=True)
    rstd_rows = lax.rsqrt(jnp.mean(center * center, axis=1, keepdims=True) + eps_norm)
    normed = center * rstd_rows
    return (normed * gain + shift, normed, rstd_rows)


def norm_backward(grad_rows, normed, rstd_rows, gain):
    scaled = grad_rows * gain
    inner = (
        scaled
        - jnp.mean(scaled, axis=1, keepdims=True)
        - normed * jnp.mean(scaled * normed, axis=1, keepdims=True)
    )
    return (rstd_rows * inner, jnp.sum(grad_rows * normed, axis=0), jnp.sum(grad_rows, axis=0))


def gelu_value(hidden_pre):
    return 0.5 * hidden_pre * (1.0 + lax.erf(hidden_pre * root_half))


def gelu_slope(hidden_pre):
    return (
        0.5 * (1.0 + lax.erf(hidden_pre * root_half))
        + hidden_pre * jnp.exp(-0.5 * hidden_pre * hidden_pre) * inv_root_two_pi
    )


def attend_forward(queries, key_rows, values, key_valid, score_scale):
    length = queries.shape[0]
    block_rows = min(512, length)
    query_blocks = queries.reshape((length // block_rows, block_rows) + queries.shape[1:])

    def one_block(query_block):
        scores = (
            jnp.einsum("qshe,kshe->shqk", query_block, key_rows, preferred_element_type=jnp.float32)
            * score_scale
        )
        scores = jnp.where(key_valid[:, None, None, :], scores, negative_fill)
        row_top = jnp.max(scores, axis=3, keepdims=True)
        exponent = jnp.exp(scores - row_top)
        row_total = jnp.sum(exponent, axis=3, keepdims=True)
        probs_low = (exponent / row_total).astype(jnp.bfloat16)
        context = jnp.einsum(
            "shqk,kshe->qshe", probs_low, values, preferred_element_type=jnp.float32
        )
        return (context.astype(jnp.bfloat16), (row_top + jnp.log(row_total))[..., 0])

    context, lse_rows = lax.map(one_block, query_blocks)
    return (context.reshape(queries.shape), lse_rows)


def attend_backward(queries, key_rows, values, grad_context, lse_rows, key_valid, score_scale):
    length = queries.shape[0]
    block_rows = min(512, length)
    block_shape = (length // block_rows, block_rows) + queries.shape[1:]

    def one_block(carry, pieces):
        grad_keys, grad_values = carry
        query_block, grad_block, lse_block = pieces
        scores = (
            jnp.einsum("qshe,kshe->shqk", query_block, key_rows, preferred_element_type=jnp.float32)
            * score_scale
        )
        scores = jnp.where(key_valid[:, None, None, :], scores, negative_fill)
        probs = jnp.exp(scores - lse_block[..., None])
        grad_values = grad_values + jnp.einsum(
            "shqk,qshe->kshe",
            probs.astype(jnp.bfloat16),
            grad_block,
            preferred_element_type=jnp.float32,
        )
        grad_probs = jnp.einsum(
            "qshe,kshe->shqk", grad_block, values, preferred_element_type=jnp.float32
        )
        inner = jnp.sum(probs * grad_probs, axis=3, keepdims=True)
        grad_scores = (probs * (grad_probs - inner) * score_scale).astype(jnp.bfloat16)
        grad_query = jnp.einsum(
            "shqk,kshe->qshe", grad_scores, key_rows, preferred_element_type=jnp.float32
        )
        grad_keys = grad_keys + jnp.einsum(
            "shqk,qshe->kshe", grad_scores, query_block, preferred_element_type=jnp.float32
        )
        return ((grad_keys, grad_values), grad_query)

    zero_rows = jnp.zeros(key_rows.shape, jnp.float32)
    pieces = (queries.reshape(block_shape), grad_context.reshape(block_shape), lse_rows)
    (grad_keys, grad_values), grad_queries = lax.scan(one_block, (zero_rows, zero_rows), pieces)
    return (grad_queries.reshape(queries.shape), grad_keys, grad_values)


def local(
    tokens,
    cotangent,
    lengths,
    deal_order,
    attn_in,
    attn_out,
    ffn_in,
    ffn_out,
    attn_bias,
    ffn_bias,
    norm_gain,
    shifts,
):
    group_count = lax.axis_size("dp")
    local_seqs = tokens.shape[2] // group_count
    dealt_tokens = jnp.take(tokens, deal_order, axis=2)
    dealt_cot = jnp.take(cotangent, deal_order, axis=2)
    arrived, arrived_cot = (
        lax.all_to_all(dealt_tokens, "dp", split_axis=2, concat_axis=1, tiled=True),
        lax.all_to_all(dealt_cot, "dp", split_axis=2, concat_axis=1, tiled=True),
    )
    half_len = arrived.shape[1]
    model_width = arrived.shape[3]
    tensor_size = lax.axis_size("mp")
    tensor_rank = lax.axis_index("mp")
    seq_len = half_len * tensor_size
    local_rows = half_len * local_seqs
    own_seqs = lax.dynamic_slice_in_dim(deal_order, lax.axis_index("dp") * local_seqs, local_seqs)
    own_lengths = jnp.take(lengths, own_seqs)
    key_valid = jnp.arange(seq_len, dtype=jnp.int32)[None, :] < own_lengths[:, None]
    head_cols = attn_in.shape[3]
    hidden_cols = ffn_in.shape[2]
    head_count = head_cols // HEAD_DIM
    score_scale = HEAD_DIM ** (-0.5)
    layers_total = norm_gain.shape[0]
    shaped = (seq_len, local_seqs, head_count, HEAD_DIM)
    flat_shape = (seq_len * local_seqs, head_cols)

    def layer_vectors(which_layer):
        bias_pair = lax.dynamic_slice_in_dim(
            attn_bias[which_layer].astype(jnp.float32), tensor_rank * head_cols, head_cols, 1
        )
        bias_up = lax.dynamic_slice_in_dim(
            ffn_bias[which_layer].astype(jnp.float32), tensor_rank * hidden_cols, hidden_cols, 0
        )
        return (
            bias_pair,
            bias_up,
            norm_gain[which_layer].astype(jnp.float32),
            shifts[which_layer].astype(jnp.float32),
        )

    hidden_rows = arrived.reshape(local_rows, model_width).astype(jnp.float32)
    weights_all = []
    which_layer = 0
    w_three, w_back, w_up, w_down = fetch_weights(
        attn_in[which_layer], attn_out[which_layer], ffn_in[which_layer], ffn_out[which_layer]
    )
    bias_pair, bias_up, gain_pair, shift_four = layer_vectors(which_layer)
    wide_rows = gather_rows(hidden_rows.astype(jnp.bfloat16))
    projected = jnp.einsum("rd,cde->cre", wide_rows, w_three, preferred_element_type=jnp.float32)
    queries = (projected[0] + bias_pair[0]).astype(jnp.bfloat16).reshape(shaped)
    key_rows = projected[1].astype(jnp.bfloat16).reshape(shaped)
    values = (projected[2] + bias_pair[1]).astype(jnp.bfloat16).reshape(shaped)
    context, lse_rows = attend_forward(queries, key_rows, values, key_valid, score_scale)
    context_rows = context.reshape(flat_shape)

    def attn_term(offset, number, context_rows=context_rows, w_back=w_back):
        return jnp.dot(context_rows, w_back, preferred_element_type=jnp.float32)

    mixed_one = hidden_rows + spread_rows(attn_term, local_rows) + shift_four[0]
    middle, mid_normed, mid_rstd = norm_forward(mixed_one, gain_pair[0], shift_four[1])
    wide_mid = gather_rows(middle.astype(jnp.bfloat16))
    hidden_pre = jnp.dot(wide_mid, w_up, preferred_element_type=jnp.float32) + bias_up
    hidden_low = gelu_value(hidden_pre).astype(jnp.bfloat16)

    def ffn_term(offset, number, hidden_low=hidden_low, w_down=w_down):
        return jnp.dot(hidden_low, w_down, preferred_element_type=jnp.float32)

    mixed_two = middle + spread_rows(ffn_term, local_rows) + shift_four[2]
    hidden_rows, out_normed, out_rstd = norm_forward(mixed_two, gain_pair[1], shift_four[3])
    saved_all = [
        (
            wide_rows,
            queries,
            key_rows,
            values,
            context,
            lse_rows,
            mid_normed,
            mid_rstd,
            wide_mid,
            hidden_pre,
            hidden_low,
            out_normed,
            out_rstd,
        )
    ]
    weights_all.append((w_three, w_back, w_up, w_down))
    grad_state = arrived_cot.reshape(local_rows, model_width).astype(jnp.float32)
    matrix_grads = [None] * layers_total
    attn_bias_parts = [None] * layers_total
    ffn_bias_parts = [None] * layers_total
    gain_parts = [None] * layers_total
    shift_parts = [None] * layers_total
    for which_layer in reversed(range(layers_total)):
        w_three, w_back, w_up, w_down = fetch_again(
            attn_in[which_layer], attn_out[which_layer], ffn_in[which_layer], ffn_out[which_layer]
        )
        bias_pair, bias_up, gain_pair, shift_four = layer_vectors(which_layer)
        (
            wide_rows,
            queries,
            key_rows,
            values,
            context,
            lse_rows,
            mid_normed,
            mid_rstd,
            wide_mid,
            hidden_pre,
            hidden_low,
            out_normed,
            out_rstd,
        ) = saved_all[which_layer]
        grad_mixed_two, grad_gain_two, grad_shift_four = norm_backward(
            grad_state, out_normed, out_rstd, gain_pair[1]
        )
        grad_down_bias = jnp.sum(grad_mixed_two, axis=0)
        grad_down_wide = gather_grads(grad_mixed_two.astype(jnp.bfloat16))
        grad_w_down = contract_rows(hidden_low, grad_down_wide)
        grad_hidden = contract_cols(grad_down_wide, w_down) * gelu_slope(hidden_pre)
        grad_up_bias = jnp.sum(grad_hidden, axis=0)
        grad_hidden_low = grad_hidden.astype(jnp.bfloat16)
        grad_w_up = contract_rows(wide_mid, grad_hidden_low)

        def up_term(offset, number, grad_hidden_low=grad_hidden_low, w_up=w_up):
            return contract_cols(grad_hidden_low, w_up)

        grad_middle = grad_mixed_two + spread_grads(up_term, local_rows)
        grad_mixed_one, grad_gain_one, grad_shift_two = norm_backward(
            grad_middle, mid_normed, mid_rstd, gain_pair[0]
        )
        grad_out_bias = jnp.sum(grad_mixed_one, axis=0)
        grad_attn_wide = gather_grads(grad_mixed_one.astype(jnp.bfloat16))
        context_rows = context.reshape(flat_shape)
        grad_w_back = contract_rows(context_rows, grad_attn_wide)
        grad_context = contract_cols(grad_attn_wide, w_back).astype(jnp.bfloat16).reshape(shaped)
        grad_queries, grad_keys, grad_values = attend_backward(
            queries, key_rows, values, grad_context, lse_rows, key_valid, score_scale
        )
        grad_queries = grad_queries.reshape(flat_shape)
        grad_keys = grad_keys.reshape(flat_shape)
        grad_values = grad_values.reshape(flat_shape)
        grad_pair = jnp.stack([jnp.sum(grad_queries, axis=0), jnp.sum(grad_values, axis=0)])
        grad_projected = jnp.stack([grad_queries, grad_keys, grad_values]).astype(jnp.bfloat16)
        grad_w_three = jnp.einsum(
            "rd,cre->cde", wide_rows, grad_projected, preferred_element_type=jnp.float32
        )

        def three_term(offset, number, grad_projected=grad_projected, w_three=w_three):
            return jnp.einsum(
                "cre,cde->rd", grad_projected, w_three, preferred_element_type=jnp.float32
            )

        grad_state = grad_mixed_one + spread_grads(three_term, local_rows)
        matrix_grads[which_layer] = (
            lax.psum_scatter(grad_w_three, "dp", scatter_dimension=1, tiled=True),
            lax.psum_scatter(grad_w_back, "dp", scatter_dimension=1, tiled=True),
            lax.psum_scatter(grad_w_up, "dp", scatter_dimension=0, tiled=True),
            lax.psum_scatter(grad_w_down, "dp", scatter_dimension=1, tiled=True),
        )
        attn_bias_parts[which_layer] = lax.dynamic_update_slice_in_dim(
            jnp.zeros((2, model_width), jnp.float32), grad_pair, tensor_rank * head_cols, 1
        )
        ffn_bias_parts[which_layer] = lax.dynamic_update_slice_in_dim(
            jnp.zeros((hidden_cols * tensor_size,), jnp.float32),
            grad_up_bias,
            tensor_rank * hidden_cols,
            0,
        )
        gain_parts[which_layer] = jnp.stack([grad_gain_one, grad_gain_two])
        shift_parts[which_layer] = jnp.stack(
            [grad_out_bias, grad_shift_two, grad_down_bias, grad_shift_four]
        )
    three_out, back_out, up_out, down_out = [
        jnp.stack([entry[member] for entry in matrix_grads]) for member in range(4)
    ]
    attn_bias_out, ffn_bias_out, gain_out, shift_out = lax.psum(
        (
            jnp.stack(attn_bias_parts),
            jnp.stack(ffn_bias_parts),
            jnp.stack(gain_parts),
            jnp.stack(shift_parts),
        ),
        ("dp", "mp"),
    )
    result_rows = hidden_rows.astype(jnp.bfloat16).reshape(1, half_len, local_seqs, model_width)
    result_grad = grad_state.astype(jnp.bfloat16).reshape(1, half_len, local_seqs, model_width)
    out_tokens, out_grad = (
        lax.all_to_all(result_rows, "dp", split_axis=1, concat_axis=2, tiled=True),
        lax.all_to_all(result_grad, "dp", split_axis=1, concat_axis=2, tiled=True),
    )
    return (
        out_tokens,
        out_grad,
        three_out,
        back_out,
        up_out,
        down_out,
        attn_bias_out,
        ffn_bias_out,
        gain_out,
        shift_out,
    )


def solution(mesh):
    placed = (
        P("mp", "dp", None, None),
        P("mp", "dp", None, None),
        P(),
        P(),
        P(None, None, "dp", "mp"),
        P(None, "mp", "dp"),
        P(None, "dp", "mp"),
        P(None, "mp", "dp"),
        P(),
        P(),
        P(),
        P(),
    )
    return jax.shard_map(
        local,
        mesh=mesh,
        in_specs=placed,
        out_specs=(
            P("mp", "dp", None, None),
            P("mp", "dp", None, None),
            P(None, None, "dp", "mp"),
            P(None, "mp", "dp"),
            P(None, "dp", "mp"),
            P(None, "mp", "dp"),
            P(),
            P(),
            P(),
            P(),
        ),
        check_vma=False,
    )
```

profile of v0, /device:TPU:0, one launch (start us, length us, event | category | flops | bytes accessed | tf_op | source)
XLA Modules:
  0.0 1211.0 jit_solution(1221424867472361412)
XLA Ops:
  12.6 29.6 %all_to_all.60 = bf16[1,32,16,768]{3,1,0,2:T(8,128)(2,1)} all-to-all(bf16[1,32,16,768]{3,1,0,2:T(8,128)(2,1)S(1)} %get-tuple-element.321), channel_id=1, replica_groups=mesh['dp'=16,'mp'=2] {'dp'}, dimensions={2} | all-to-all | bytes 1572864 | tf_op jit(solution)/shard_map/all_to_all | solution.py:179
  47.0 44.4 %all-gather.1 = bf16[1,384,768]{1,2,0:T(8,128)(2,1)} all-gather(bf16[1,384,48]{1,2,0:T(8,128)(2,1)S(1)} %copy-done.25), channel_id=3, replica_groups=mesh['dp'=16,'mp'=2] {'dp'}, dimensions={2}, use_global_device_ids=true | all-gather | bytes 626688 | tf_op jit(solution)/shard_map/all_gather | solution.py:42
  91.5 22.1 %all-gather.20.cloned.1.call-done = bf16[1,3,768,384]{3,2,1,0:T(8,128)(2,1)} async-done(((bf16[1,3,48,384]{3,2,1,0:T(8,128)(2,1)}), bf16[1,3,768,384]{3,2,1,0:T(8,128)(2,1)}) %all-gather.20.cloned.1.call-update) | async-done | bytes 1769488 | tf_op jit(solution)/shard_map/all_gather | solution.py:41
  123.9 18.0 %while.29 = (s32[]{:T(128)}, bf16[2,512,1,6,64]{1,4,3,2,0:T(8,128)(2,1)S(1)}, f32[2,1,6,512]{3,2,1,0:T(8,128)S(1)}, bf16[2,512,1,6,64]{1,4,3,2,0:T(8,128)(2,1)S(...) while((s32[]{:T(128)}, ...), condition=%wide.region_3.5_spmd.clone, body=%wide.region_0.4_spmd.clone.sunk | while | flops 843249664 | bytes 40231020 | solution.py:117
  158.1 62.5 %all-gather.22.cloned.1.call-done = bf16[1,768,1536]{2,1,0:T(8,128)(2,1)} async-done(((bf16[1,48,1536]{2,1,0:T(8,128)(2,1)}), bf16[1,768,1536]{2,1,0:T(8,128)(2,1)}) %all-gather.22.cloned.1.call-update) | async-done | bytes 2359312 | tf_op jit(solution)/shard_map/all_gather | solution.py:43
  220.6 10.7 all-gather.14.cloned.1.call-done
  238.4 59.4 %all-gather.24.cloned.1.call-done = bf16[1,1536,768]{1,2,0:T(8,128)(2,1)} async-done(((bf16[1,1536,48]{1,2,0:T(8,128)(2,1)}), bf16[1,1536,768]{1,2,0:T(8,128)(2,1)}) %all-gather.24.cloned.1.call-update) | async-done | bytes 2359312 | tf_op jit(solution)/shard_map/all_gather | solution.py:44
  304.4 25.7 %all_to_all.61 = bf16[1,32,16,768]{3,1,0,2:T(8,128)(2,1)S(1)} all-to-all(bf16[1,32,16,768]{3,1,0,2:T(8,128)(2,1)} %get-tuple-element.320), channel_id=1, replica_groups=mesh['dp'=16,'mp'=2] {'dp'}, dimensions={2} | all-to-all | bytes 1572864 | tf_op jit(solution)/shard_map/all_to_all | solution.py:180
  338.0 7.7 all-gather.16.cloned.1.call-done
  345.7 7.7 fusion.141
  358.9 10.3 reduce-scatter.12.cloned.1.call-done
  376.3 11.1 all-gather.18.cloned.1.call-done
  392.7 163.6 %while.30 = (s32[]{:T(128)}, f32[1024,1,6,64]{0,3,2,1:T(8,128)}, f32[1024,1,6,64]{0,3,2,1:T(8,128)}, f32[2,512,1,6,64]{1,4,3,2,0:T(8,128)}, bf16[2,512,1,6,64]{1...) while((s32[]{:T(128)}, f32[1024,1,6,64]{0,3,2,1:T(8,128)}, ...), condition=%wide.region_17.19_spmd.clone, body=%wide.region_15.18_spmd.clone.sunk | while | flops 2096636928 | bytes 199866560 | solution.py:156
  406.1 34.3 %bitcast_add_fusion.4 = f32[1024,1,6,64]{0,3,2,1:T(8,128)} fusion(f32[1024,1,6,64]{0,3,2,1:T(8,128)} %get-tuple-element.475, f32[6,512,1024]{2,1,0:T(8,128)} %fusion.187, f32[6,512,1024]{2,1,0:T(8,128)} %copy-done, f32[6,512]{1,0:T(8,128)S(1)} %dynamic-slice_bitcast_fusion.3, pred[1024]{0:T(1024)(128)(4,1)S(1)} %compare_reduce_fusion.5, ...), kind=kOutput, calls=%fused_computation.42.clone.1 | convolution fusion | flops 438046720 | bytes 53905412 | tf_op jit(solution)/shard_map/while/body/eval_jaxpr/shqk,qshe->kshe/dot_general | solution.py:149
  440.4 33.6 %fusion.189 = f32[2,512,1,6,64]{1,4,3,2,0:T(8,128)} fusion(f32[2,512,1,6,64]{1,4,3,2,0:T(8,128)} %get-tuple-element.477, s32[]{:T(128)S(6)} %copy.127, f32[6,512,1024]{2,1,0:T(8,128)} %fusion.187, f32[6,512,1024]{2,1,0:T(8,128)} %copy-done, f32[6,512]{1,0:T(8,128)S(1)} %dynamic-slice_bitcast_fusion.3, pred[1024]{0:T(1024)(128)(4,1)S(1)} %compare_reduce_fusion.5, ...), kind=kOutput, calls=%fused_computation.44.clone.1 | convolution fusion | flops 437260288 | bytes 51939332 | tf_op jit(solution)/shard_map/while/body/eval_jaxpr/shqk,kshe->qshe/dot_general | solution.py:146
  488.0 34.5 %bitcast_add_fusion.4 = f32[1024,1,6,64]{0,3,2,1:T(8,128)} fusion(f32[1024,1,6,64]{0,3,2,1:T(8,128)} %get-tuple-element.475, f32[6,512,1024]{2,1,0:T(8,128)} %fusion.187, f32[6,512,1024]{2,1,0:T(8,128)} %copy-done, f32[6,512]{1,0:T(8,128)S(1)} %dynamic-slice_bitcast_fusion.3, pred[1024]{0:T(1024)(128)(4,1)S(1)} %compare_reduce_fusion.5, ...), kind=kOutput, calls=%fused_computation.42.clone.1 | convolution fusion | flops 438046720 | bytes 53905412 | tf_op jit(solution)/shard_map/while/body/eval_jaxpr/shqk,qshe->kshe/dot_general | solution.py:149
  522.6 33.6 %fusion.189 = f32[2,512,1,6,64]{1,4,3,2,0:T(8,128)} fusion(f32[2,512,1,6,64]{1,4,3,2,0:T(8,128)} %get-tuple-element.477, s32[]{:T(128)S(6)} %copy.127, f32[6,512,1024]{2,1,0:T(8,128)} %fusion.187, f32[6,512,1024]{2,1,0:T(8,128)} %copy-done, f32[6,512]{1,0:T(8,128)S(1)} %dynamic-slice_bitcast_fusion.3, pred[1024]{0:T(1024)(128)(4,1)S(1)} %compare_reduce_fusion.5, ...), kind=kOutput, calls=%fused_computation.44.clone.1 | convolution fusion | flops 437260288 | bytes 51939332 | tf_op jit(solution)/shard_map/while/body/eval_jaxpr/shqk,kshe->qshe/dot_general | solution.py:146
  622.8 22.3 %all-to-all-done.1 = bf16[16,2,12288]{2,1,0:T(2,128)(2,1)S(1)} async-done(((bf16[16,2,12288]{2,1,0:T(2,128)(2,1)}), bf16[16,2,12288]{2,1,0:T(2,128)(2,1)S(1)}, u32[]{:S(2)}, u32[]{:S(2)}) %all-to-all-start.1) | async-done | bytes 786464 | tf_op jit(solution)/shard_map/all_to_all | solution.py:361
  645.1 9.7 all-to-all-start.3
  658.8 46.7 %all-reduce.1 = (f32[1,2,768]{2,1,0:T(2,128)}, f32[1,3072]{1,0:T(1,128)}, f32[1,2,768]{2,1,0:T(2,128)}, f32[1,4,768]{2,1,0:T(4,128)}) all-reduce(f32[1,2,768]{2,1,0:T(2,128)S(1)} %fusion.130, f32[1,3072]{1,0:T(1,128)S(1)} %reshape_dynamic-update-slice_fusion, ...), channel_id=1, replica_groups=mesh['dp'=16,'mp'=2] {'dp','mp'}, use_global_device_ids=true, to_apply=%region_25.27 | all-reduce | flops 9216 | bytes 73728 | tf_op jit(solution)/shard_map/psum | solution.py:349
  705.5 85.9 %all-reduce.4.cloned.1.call-done = f32[3,768,384]{2,0,1:T(4,128)} async-done(((f32[3,768,384]{2,0,1:T(4,128)}), f32[3,768,384]{2,0,1:T(4,128)}) %all-reduce.4.cloned.1.call-update) | async-done | bytes 3538960
  795.3 124.7 %reduce-scatter.16.cloned.1.call-done = f32[384,48]{0,1:T(8,128)} async-done(((f32[384,768]{0,1:T(8,128)}), f32[384,48]{0,1:T(8,128)}) %reduce-scatter.16.cloned.1.call-update) | async-done | bytes 73744 | tf_op jit(solution)/shard_map/reduce_scatter | solution.py:329
  920.1 142.5 %reduce-scatter.20.cloned.1.call-done = f32[1536,48]{0,1:T(8,128)} async-done(((f32[1536,768]{0,1:T(8,128)}), f32[1536,48]{0,1:T(8,128)}) %reduce-scatter.20.cloned.1.call-update) | async-done | bytes 294928 | tf_op jit(solution)/shard_map/reduce_scatter | solution.py:331
  1062.6 141.7 %reduce-scatter.18.cloned.1.call-done = f32[48,1536]{1,0:T(8,128)} async-done(((f32[768,1536]{1,0:T(8,128)}), f32[48,1536]{1,0:T(8,128)}) %reduce-scatter.18.cloned.1.call-update) | async-done | bytes 294928 | tf_op jit(solution)/shard_map/reduce_scatter | solution.py:330
  (245 shorter events, 191.5 us)
Async XLA Ops:
  7.2 84.3 %all-gather.12.cloned.1.call-start = ((), (), s32[]{:S(2)}) async-start(), calls=%async_computation.11 | async-start | bytes 2359296 | tf_op jit(solution)/shard_map/all_gather | solution.py:14
  12.5 30.5 %copy-start.38 = (s32[16]{0:T(128)S(1)}, s32[16]{0:T(128)}, u32[]{:S(2)}) copy-start(s32[16]{0:T(128)} %param.21) | copy-start | bytes 196
  12.5 33.0 %copy-start.35 = (bf16[1,2,768]{2,1,0:T(2,128)(2,1)S(1)}, bf16[1,2,768]{2,1,0:T(2,128)(2,1)}, u32[]{:S(2)}) copy-start(bf16[1,2,768]{2,1,0:T(2,128)(2,1)} %param.26) | copy-start | bytes 9220
  12.5 33.2 %copy-start.39 = (s32[16]{0:T(128)S(1)}, s32[16]{0:T(128)}, u32[]{:S(2)}) copy-start(s32[16]{0:T(128)} %param.20) | copy-start | bytes 196
  12.5 34.5 %copy-start.25 = (bf16[1,384,48]{1,2,0:T(8,128)(2,1)S(1)}, bf16[1,384,48]{1,2,0:T(8,128)(2,1)}, u32[]{:S(2)}) copy-start(bf16[1,384,48]{1,2,0:T(8,128)(2,1)} %param.23) | copy-start | bytes 110596
  42.2 71.4 %all-gather.20.cloned.1.call-start = ((), (), s32[]{:S(2)}) async-start(), calls=%async_computation.22 | async-start | bytes 1880064 | tf_op jit(solution)/shard_map/all_gather | solution.py:41
  43.0 111.0 %reduce-scatter.8.cloned.1.call-start = ((), (), s32[]{:S(2)}) async-start(), calls=%async_computation.12 | async-start | bytes 2359296 | tf_op jit(solution)/shard_map/reduce_scatter | solution.py:22
  146.0 74.5 %all-gather.22.cloned.1.call-start = ((), (), s32[]{:S(2)}) async-start(), calls=%async_computation.23 | async-start | bytes 2506752 | tf_op jit(solution)/shard_map/all_gather | solution.py:43
  146.6 84.7 %all-gather.14.cloned.1.call-start = ((), (), s32[]{:S(2)}) async-start(), calls=%async_computation.13 | async-start | bytes 2359296 | tf_op jit(solution)/shard_map/all_gather | solution.py:14
  157.4 140.4 %all-gather.24.cloned.1.call-start = ((), (), s32[]{:S(2)}) async-start(), calls=%async_computation.24 | async-start | bytes 2506752 | tf_op jit(solution)/shard_map/all_gather | solution.py:44
  158.0 173.3 %reduce-scatter.10.cloned.1.call-start = ((), (), s32[]{:S(2)}) async-start(), calls=%async_computation.14 | async-start | bytes 2359296 | tf_op jit(solution)/shard_map/reduce_scatter | solution.py:22
  304.3 41.4 %all-gather.16.cloned.1.call-start = ((), (), s32[]{:S(2)}) async-start(), calls=%async_computation.15 | async-start | bytes 2359296 | tf_op jit(solution)/shard_map/all_gather | solution.py:18
  338.0 31.3 %reduce-scatter.12.cloned.1.call-start = ((), (), s32[]{:S(2)}) async-start(), calls=%async_computation.16 | async-start | bytes 2359296 | tf_op jit(solution)/shard_map/reduce_scatter | solution.py:31
  358.9 28.5 %all-gather.18.cloned.1.call-start = ((), (), s32[]{:S(2)}) async-start(), calls=%async_computation.17 | async-start | bytes 2359296 | tf_op jit(solution)/shard_map/all_gather | solution.py:18
  376.2 237.5 %reduce-scatter.14.cloned.1.call-start = ((), (), s32[]{:S(2)}) async-start(), calls=%async_computation.18 | async-start | bytes 2359296 | tf_op jit(solution)/shard_map/reduce_scatter | solution.py:31
  569.5 222.0 %all-reduce.4.cloned.1.call-start = ((), (), s32[]{:S(2)}) async-start(), calls=%async_computation.25 | async-start | bytes 9437184
  577.8 342.2 %reduce-scatter.16.cloned.1.call-start = ((), (), s32[]{:S(2)}) async-start(), calls=%async_computation.19 | async-start | bytes 1253376 | tf_op jit(solution)/shard_map/reduce_scatter | solution.py:329
  582.5 480.1 %reduce-scatter.20.cloned.1.call-start = ((), (), s32[]{:S(2)}) async-start(), calls=%async_computation.21 | async-start | bytes 5013504 | tf_op jit(solution)/shard_map/reduce_scatter | solution.py:331
  588.9 615.4 %reduce-scatter.18.cloned.1.call-start = ((), (), s32[]{:S(2)}) async-start(), calls=%async_computation.20 | async-start | bytes 5013504 | tf_op jit(solution)/shard_map/reduce_scatter | solution.py:330
  606.8 38.3 %all-to-all-start.1 = ((bf16[16,2,12288]{2,1,0:T(2,128)(2,1)}), bf16[16,2,12288]{2,1,0:T(2,128)(2,1)S(1)}, u32[]{:S(2)}, u32[]{:S(2)}) async-start(bf16[16,2,12288]{2,1,0:T(2,128)(2,1)} %reshape.397), calls=%async_computation.3 | async-start | bytes 1572864 | tf_op jit(solution)/shard_map/all_to_all | solution.py:361
  621.6 33.1 %copy-start.40 = (u32[32]{0:T(128)S(1)}, u32[32]{0:T(128)}, u32[]{:S(2)}) copy-start(u32[32]{0:T(128)} %constant.142) | copy-start | bytes 388
  621.7 34.3 %copy-start.7 = (bf16[1,32,16,768]{3,1,0,2:T(8,128)(2,1)S(1)}, bf16[1,32,16,768]{3,1,0,2:T(8,128)(2,1)}, u32[]{:S(2)}) copy-start(bf16[1,32,16,768]{3,1,0,2:T(8,128)(2,1)} %copy-done.5) | copy-start | bytes 2359300
  622.8 33.4 %copy-start.26 = (f32[768]{0:T(1024)S(1)}, f32[768]{0:T(1024)}, u32[]{:S(2)}) copy-start(f32[768]{0:T(1024)} %get-tuple-element.255) | copy-start | bytes 9220
  645.1 148.1 %all-to-all-start.3 = ((bf16[16,2,12288]{2,1,0:T(2,128)(2,1)}), bf16[16,2,12288]{2,1,0:T(2,128)(2,1)S(1)}, u32[]{:S(2)}, u32[]{:S(2)}) async-start(bf16[16,2,12288]{2,1,0:T(2,128)(2,1)} %reshape.399), calls=%async_computation.7 | async-start | bytes 1572864 | tf_op jit(solution)/shard_map/all_to_all | solution.py:362
  (35 other events, 106.2 us)
Sparse Core Ops, SparseCore 0:
  42.3 7.5 all-gather.11
  52.6 60.9 all-gather.19
  146.1 7.8 reduce-scatter.7
  157.0 63.4 all-gather.21
  222.6 8.6 all-gather.13
  234.3 63.4 all-gather.23
  304.4 7.8 reduce-scatter.9
  338.1 7.5 all-gather.15
  359.0 10.2 reduce-scatter.11
  376.3 10.9 all-gather.17
  569.6 10.1 reduce-scatter.13
  585.4 205.9 all-reduce.3
  797.5 122.5 reduce-scatter.15
  926.5 136.0 reduce-scatter.19
  1068.2 136.0 reduce-scatter.17
where the time goes:
time: 1220 us; the launch traced here: 1210 us
  waiting for transfers between devices  710 us (58%)
  matrix products  234 us (19%)
  blocking collectives  147 us (12%)
  other arithmetic  42.7 us (4%)
  local copies, waits for them, and re-layouts  41.3 us (3%)
  between operations  18.2 us (1%)
  starting transfers between devices  17.6 us (1%)
    reduce_scatter x1, waiting for transfers between devices, local(): lax.psum_scatter(grad_w_down, 'dp', scatter_dimension=1, tiled=True)  143 us
    reduce_scatter x1, waiting for transfers between devices, local(): lax.psum_scatter(grad_w_up, 'dp', scatter_dimension=0, tiled=True)  142 us
    reduce_scatter x1, waiting for transfers between devices, local(): lax.psum_scatter(grad_w_back, 'dp', scatter_dimension=1, tiled=True)  125 us
    unnamed x16, waiting for transfers between devices  87.9 us
    dot_general x2, matrix products, one_block(): jnp.einsum('shqk,qshe->kshe', grad_scores, query_block, preferred_element...  68.8 us
    dot_general x2, matrix products, one_block(): jnp.einsum('shqk,kshe->qshe', grad_scores, key_rows, preferred_element_ty...  67.1 us
    all_gather x1, waiting for transfers between devices, fetch_weights(): lax.all_gather(up_part, 'dp', axis=0, tiled=True)  62.5 us
    all_gather x1, waiting for transfers between devices, fetch_weights(): lax.all_gather(down_part, 'dp', axis=1, tiled=True)  59.4 us
  transfers between devices with their start and end apart: 17, of which 13 were waited for; matrix products, arithmetic and copies ran while one was open for 5% of the time, Pallas kernels for 0%

commit v1 on v0

--- a/solution.py
+++ b/solution.py
@@ -347,13 +347,16 @@
         jnp.stack([entry[member] for entry in matrix_grads]) for member in range(4)
     ]
     attn_bias_out, ffn_bias_out, gain_out, shift_out = lax.psum(
-        (
-            jnp.stack(attn_bias_parts),
-            jnp.stack(ffn_bias_parts),
-            jnp.stack(gain_parts),
-            jnp.stack(shift_parts),
+        lax.psum(
+            (
+                jnp.stack(attn_bias_parts),
+                jnp.stack(ffn_bias_parts),
+                jnp.stack(gain_parts),
+                jnp.stack(shift_parts),
+            ),
+            "mp",
         ),
-        ("dp", "mp"),
+        "dp",
     )
     result_rows = hidden_rows.astype(jnp.bfloat16).reshape(1, half_len, local_seqs, model_width)
     result_grad = grad_state.astype(jnp.bfloat16).reshape(1, half_len, local_seqs, model_width)

time: 1220 us -> 1220 us (level)
  blocking collectives: 147 us -> 188 us
  waiting for transfers between devices: 710 us -> 669 us
    psum x0 -> x1, blocking collectives: none -> 84.9 us  [local(): lax.psum(lax.psum((jnp.stack(attn_bias_parts), jnp.stack(ffn_bias_parts),...]
    psum x1, blocking collectives: 46.7 us -> 3.49 us  [local(): lax.psum((jnp.stack(attn_bias_parts), jnp.stack(ffn_bias_parts), jnp.stac...]
    unnamed x16, waiting for transfers between devices: 87.9 us -> 46.3 us
where the time goes in v1:
time: 1220 us; the launch traced here: 1210 us
  waiting for transfers between devices  669 us (55%)
  matrix products  234 us (19%)
  blocking collectives  188 us (15%)
  other arithmetic  42.7 us (4%)
  local copies, waits for them, and re-layouts  41.3 us (3%)
  between operations  18.2 us (1%)
  starting transfers between devices  17.6 us (1%)
    reduce_scatter x1, waiting for transfers between devices, local(): lax.psum_scatter(grad_w_down, 'dp', scatter_dimension=1, tiled=True)  143 us
    reduce_scatter x1, waiting for transfers between devices, local(): lax.psum_scatter(grad_w_up, 'dp', scatter_dimension=0, tiled=True)  142 us
    reduce_scatter x1, waiting for transfers between devices, local(): lax.psum_scatter(grad_w_back, 'dp', scatter_dimension=1, tiled=True)  125 us
    psum x1, blocking collectives, local(): lax.psum(lax.psum((jnp.stack(attn_bias_parts), jnp.stack(ffn_bias_parts),...  84.9 us
    dot_general x2, matrix products, one_block(): jnp.einsum('shqk,qshe->kshe', grad_scores, query_block, preferred_element...  68.8 us
    dot_general x2, matrix products, one_block(): jnp.einsum('shqk,kshe->qshe', grad_scores, key_rows, preferred_element_ty...  67.1 us
    all_gather x1, waiting for transfers between devices, fetch_weights(): lax.all_gather(up_part, 'dp', axis=0, tiled=True)  62.5 us
    all_gather x1, waiting for transfers between devices, fetch_weights(): lax.all_gather(down_part, 'dp', axis=1, tiled=True)  59.4 us
  transfers between devices with their start and end apart: 17, of which 13 were waited for; matrix products, arithmetic and copies ran while one was open for 5% of the time, Pallas kernels for 0%

profile of v1, /device:TPU:0, one launch (start us, length us, event | category | flops | bytes accessed | tf_op | source)
XLA Modules:
  0.0 1211.8 jit_solution(11907624497094423256)
XLA Ops:
  12.6 29.6 %all_to_all.60 = bf16[1,32,16,768]{3,1,0,2:T(8,128)(2,1)} all-to-all(bf16[1,32,16,768]{3,1,0,2:T(8,128)(2,1)S(1)} %get-tuple-element.325), channel_id=1, replica_groups=mesh['dp'=16,'mp'=2] {'dp'}, dimensions={2} | all-to-all | bytes 1572864 | tf_op jit(solution)/shard_map/all_to_all | solution.py:179
  47.0 44.4 %all-gather.1 = bf16[1,384,768]{1,2,0:T(8,128)(2,1)} all-gather(bf16[1,384,48]{1,2,0:T(8,128)(2,1)S(1)} %copy-done.25), channel_id=3, replica_groups=mesh['dp'=16,'mp'=2] {'dp'}, dimensions={2}, use_global_device_ids=true | all-gather | bytes 626688 | tf_op jit(solution)/shard_map/all_gather | solution.py:42
  91.5 22.1 %all-gather.20.cloned.1.call-done = bf16[1,3,768,384]{3,2,1,0:T(8,128)(2,1)} async-done(((bf16[1,3,48,384]{3,2,1,0:T(8,128)(2,1)}), bf16[1,3,768,384]{3,2,1,0:T(8,128)(2,1)}) %all-gather.20.cloned.1.call-update) | async-done | bytes 1769488 | tf_op jit(solution)/shard_map/all_gather | solution.py:41
  123.9 18.0 %while.29 = (s32[]{:T(128)}, bf16[2,512,1,6,64]{1,4,3,2,0:T(8,128)(2,1)S(1)}, f32[2,1,6,512]{3,2,1,0:T(8,128)S(1)}, bf16[2,512,1,6,64]{1,4,3,2,0:T(8,128)(2,1)S(...) while((s32[]{:T(128)}, ...), condition=%wide.region_3.5_spmd.clone, body=%wide.region_0.4_spmd.clone.sunk | while | flops 843249664 | bytes 40231020 | solution.py:117
  158.1 62.5 %all-gather.22.cloned.1.call-done = bf16[1,768,1536]{2,1,0:T(8,128)(2,1)} async-done(((bf16[1,48,1536]{2,1,0:T(8,128)(2,1)}), bf16[1,768,1536]{2,1,0:T(8,128)(2,1)}) %all-gather.22.cloned.1.call-update) | async-done | bytes 2359312 | tf_op jit(solution)/shard_map/all_gather | solution.py:43
  220.6 10.7 all-gather.14.cloned.1.call-done
  238.4 59.4 %all-gather.24.cloned.1.call-done = bf16[1,1536,768]{1,2,0:T(8,128)(2,1)} async-done(((bf16[1,1536,48]{1,2,0:T(8,128)(2,1)}), bf16[1,1536,768]{1,2,0:T(8,128)(2,1)}) %all-gather.24.cloned.1.call-update) | async-done | bytes 2359312 | tf_op jit(solution)/shard_map/all_gather | solution.py:44
  304.4 25.7 %all_to_all.61 = bf16[1,32,16,768]{3,1,0,2:T(8,128)(2,1)S(1)} all-to-all(bf16[1,32,16,768]{3,1,0,2:T(8,128)(2,1)} %get-tuple-element.324), channel_id=1, replica_groups=mesh['dp'=16,'mp'=2] {'dp'}, dimensions={2} | all-to-all | bytes 1572864 | tf_op jit(solution)/shard_map/all_to_all | solution.py:180
  338.0 7.7 all-gather.16.cloned.1.call-done
  345.7 7.7 fusion.141
  358.9 10.3 reduce-scatter.12.cloned.1.call-done
  376.3 11.1 all-gather.18.cloned.1.call-done
  392.7 163.6 %while.30 = (s32[]{:T(128)}, f32[1024,1,6,64]{0,3,2,1:T(8,128)}, f32[1024,1,6,64]{0,3,2,1:T(8,128)}, f32[2,512,1,6,64]{1,4,3,2,0:T(8,128)}, bf16[2,512,1,6,64]{1...) while((s32[]{:T(128)}, f32[1024,1,6,64]{0,3,2,1:T(8,128)}, ...), condition=%wide.region_17.19_spmd.clone, body=%wide.region_15.18_spmd.clone.sunk | while | flops 2096636928 | bytes 199866560 | solution.py:156
  406.1 34.3 %bitcast_add_fusion.4 = f32[1024,1,6,64]{0,3,2,1:T(8,128)} fusion(f32[1024,1,6,64]{0,3,2,1:T(8,128)} %get-tuple-element.479, f32[6,512,1024]{2,1,0:T(8,128)} %fusion.187, f32[6,512,1024]{2,1,0:T(8,128)} %copy-done, f32[6,512]{1,0:T(8,128)S(1)} %dynamic-slice_bitcast_fusion.3, pred[1024]{0:T(1024)(128)(4,1)S(1)} %compare_reduce_fusion.5, ...), kind=kOutput, calls=%fused_computation.42.clone.1 | convolution fusion | flops 438046720 | bytes 53905412 | tf_op jit(solution)/shard_map/while/body/eval_jaxpr/shqk,qshe->kshe/dot_general | solution.py:149
  440.4 33.6 %fusion.189 = f32[2,512,1,6,64]{1,4,3,2,0:T(8,128)} fusion(f32[2,512,1,6,64]{1,4,3,2,0:T(8,128)} %get-tuple-element.481, s32[]{:T(128)S(6)} %copy.127, f32[6,512,1024]{2,1,0:T(8,128)} %fusion.187, f32[6,512,1024]{2,1,0:T(8,128)} %copy-done, f32[6,512]{1,0:T(8,128)S(1)} %dynamic-slice_bitcast_fusion.3, pred[1024]{0:T(1024)(128)(4,1)S(1)} %compare_reduce_fusion.5, ...), kind=kOutput, calls=%fused_computation.44.clone.1 | convolution fusion | flops 437260288 | bytes 51939332 | tf_op jit(solution)/shard_map/while/body/eval_jaxpr/shqk,kshe->qshe/dot_general | solution.py:146
  488.0 34.5 %bitcast_add_fusion.4 = f32[1024,1,6,64]{0,3,2,1:T(8,128)} fusion(f32[1024,1,6,64]{0,3,2,1:T(8,128)} %get-tuple-element.479, f32[6,512,1024]{2,1,0:T(8,128)} %fusion.187, f32[6,512,1024]{2,1,0:T(8,128)} %copy-done, f32[6,512]{1,0:T(8,128)S(1)} %dynamic-slice_bitcast_fusion.3, pred[1024]{0:T(1024)(128)(4,1)S(1)} %compare_reduce_fusion.5, ...), kind=kOutput, calls=%fused_computation.42.clone.1 | convolution fusion | flops 438046720 | bytes 53905412 | tf_op jit(solution)/shard_map/while/body/eval_jaxpr/shqk,qshe->kshe/dot_general | solution.py:149
  522.6 33.6 %fusion.189 = f32[2,512,1,6,64]{1,4,3,2,0:T(8,128)} fusion(f32[2,512,1,6,64]{1,4,3,2,0:T(8,128)} %get-tuple-element.481, s32[]{:T(128)S(6)} %copy.127, f32[6,512,1024]{2,1,0:T(8,128)} %fusion.187, f32[6,512,1024]{2,1,0:T(8,128)} %copy-done, f32[6,512]{1,0:T(8,128)S(1)} %dynamic-slice_bitcast_fusion.3, pred[1024]{0:T(1024)(128)(4,1)S(1)} %compare_reduce_fusion.5, ...), kind=kOutput, calls=%fused_computation.44.clone.1 | convolution fusion | flops 437260288 | bytes 51939332 | tf_op jit(solution)/shard_map/while/body/eval_jaxpr/shqk,kshe->qshe/dot_general | solution.py:146
  622.8 22.3 %all-to-all-done.1 = bf16[16,2,12288]{2,1,0:T(2,128)(2,1)S(1)} async-done(((bf16[16,2,12288]{2,1,0:T(2,128)(2,1)}), bf16[16,2,12288]{2,1,0:T(2,128)(2,1)S(1)}, u32[]{:S(2)}, u32[]{:S(2)}) %all-to-all-start.1) | async-done | bytes 786464 | tf_op jit(solution)/shard_map/all_to_all | solution.py:364
  645.1 9.7 all-to-all-start.3
  662.3 84.9 %all-reduce.1 = (f32[1,2,768]{2,1,0:T(2,128)}, f32[1,3072]{1,0:T(1,128)}, f32[1,2,768]{2,1,0:T(2,128)}, f32[1,4,768]{2,1,0:T(4,128)}) all-reduce(f32[1,2,768]{2,1,0:T(2,128)S(1)} %get-tuple-element.305, f32[1,3072]{1,0:T(1,128)S(1)} %get-tuple-element.306, ...), channel_id=1, replica_groups=mesh['dp'=16,'mp'=2] {'dp'}, use_global_device_ids=true, to_apply=%region_26.28 | all-reduce | flops 9216 | bytes 73728 | tf_op jit(solution)/shard_map/psum | solution.py:349
  747.2 44.4 %all-reduce.5.cloned.1.call-done = f32[3,768,384]{2,0,1:T(4,128)} async-done(((f32[3,768,384]{2,0,1:T(4,128)}), f32[3,768,384]{2,0,1:T(4,128)}) %all-reduce.5.cloned.1.call-update) | async-done | bytes 3538960
  795.5 124.7 %reduce-scatter.16.cloned.1.call-done = f32[384,48]{0,1:T(8,128)} async-done(((f32[384,768]{0,1:T(8,128)}), f32[384,48]{0,1:T(8,128)}) %reduce-scatter.16.cloned.1.call-update) | async-done | bytes 73744 | tf_op jit(solution)/shard_map/reduce_scatter | solution.py:329
  920.2 143.0 %reduce-scatter.20.cloned.1.call-done = f32[1536,48]{0,1:T(8,128)} async-done(((f32[1536,768]{0,1:T(8,128)}), f32[1536,48]{0,1:T(8,128)}) %reduce-scatter.20.cloned.1.call-update) | async-done | bytes 294928 | tf_op jit(solution)/shard_map/reduce_scatter | solution.py:331
  1063.2 141.9 %reduce-scatter.18.cloned.1.call-done = f32[48,1536]{1,0:T(8,128)} async-done(((f32[768,1536]{1,0:T(8,128)}), f32[48,1536]{1,0:T(8,128)}) %reduce-scatter.18.cloned.1.call-update) | async-done | bytes 294928 | tf_op jit(solution)/shard_map/reduce_scatter | solution.py:330
  (246 shorter events, 195.0 us)
Async XLA Ops:
  7.2 84.3 %all-gather.12.cloned.1.call-start = ((), (), s32[]{:S(2)}) async-start(), calls=%async_computation.11 | async-start | bytes 2359296 | tf_op jit(solution)/shard_map/all_gather | solution.py:14
  12.5 30.5 %copy-start.38 = (s32[16]{0:T(128)S(1)}, s32[16]{0:T(128)}, u32[]{:S(2)}) copy-start(s32[16]{0:T(128)} %param.21) | copy-start | bytes 196
  12.5 33.0 %copy-start.35 = (bf16[1,2,768]{2,1,0:T(2,128)(2,1)S(1)}, bf16[1,2,768]{2,1,0:T(2,128)(2,1)}, u32[]{:S(2)}) copy-start(bf16[1,2,768]{2,1,0:T(2,128)(2,1)} %param.26) | copy-start | bytes 9220
  12.5 33.2 %copy-start.39 = (s32[16]{0:T(128)S(1)}, s32[16]{0:T(128)}, u32[]{:S(2)}) copy-start(s32[16]{0:T(128)} %param.20) | copy-start | bytes 196
  12.5 34.5 %copy-start.25 = (bf16[1,384,48]{1,2,0:T(8,128)(2,1)S(1)}, bf16[1,384,48]{1,2,0:T(8,128)(2,1)}, u32[]{:S(2)}) copy-start(bf16[1,384,48]{1,2,0:T(8,128)(2,1)} %param.23) | copy-start | bytes 110596
  42.2 71.4 %all-gather.20.cloned.1.call-start = ((), (), s32[]{:S(2)}) async-start(), calls=%async_computation.22 | async-start | bytes 1880064 | tf_op jit(solution)/shard_map/all_gather | solution.py:41
  43.0 111.0 %reduce-scatter.8.cloned.1.call-start = ((), (), s32[]{:S(2)}) async-start(), calls=%async_computation.12 | async-start | bytes 2359296 | tf_op jit(solution)/shard_map/reduce_scatter | solution.py:22
  146.0 74.5 %all-gather.22.cloned.1.call-start = ((), (), s32[]{:S(2)}) async-start(), calls=%async_computation.23 | async-start | bytes 2506752 | tf_op jit(solution)/shard_map/all_gather | solution.py:43
  146.6 84.7 %all-gather.14.cloned.1.call-start = ((), (), s32[]{:S(2)}) async-start(), calls=%async_computation.13 | async-start | bytes 2359296 | tf_op jit(solution)/shard_map/all_gather | solution.py:14
  157.4 140.4 %all-gather.24.cloned.1.call-start = ((), (), s32[]{:S(2)}) async-start(), calls=%async_computation.24 | async-start | bytes 2506752 | tf_op jit(solution)/shard_map/all_gather | solution.py:44
  158.0 173.3 %reduce-scatter.10.cloned.1.call-start = ((), (), s32[]{:S(2)}) async-start(), calls=%async_computation.14 | async-start | bytes 2359296 | tf_op jit(solution)/shard_map/reduce_scatter | solution.py:22
  304.3 41.4 %all-gather.16.cloned.1.call-start = ((), (), s32[]{:S(2)}) async-start(), calls=%async_computation.15 | async-start | bytes 2359296 | tf_op jit(solution)/shard_map/all_gather | solution.py:18
  338.0 31.3 %reduce-scatter.12.cloned.1.call-start = ((), (), s32[]{:S(2)}) async-start(), calls=%async_computation.16 | async-start | bytes 2359296 | tf_op jit(solution)/shard_map/reduce_scatter | solution.py:31
  358.9 28.5 %all-gather.18.cloned.1.call-start = ((), (), s32[]{:S(2)}) async-start(), calls=%async_computation.17 | async-start | bytes 2359296 | tf_op jit(solution)/shard_map/all_gather | solution.py:18
  376.2 237.5 %reduce-scatter.14.cloned.1.call-start = ((), (), s32[]{:S(2)}) async-start(), calls=%async_computation.18 | async-start | bytes 2359296 | tf_op jit(solution)/shard_map/reduce_scatter | solution.py:31
  569.5 222.1 %all-reduce.5.cloned.1.call-start = ((), (), s32[]{:S(2)}) async-start(), calls=%async_computation.25 | async-start | bytes 9437184
  577.8 342.4 %reduce-scatter.16.cloned.1.call-start = ((), (), s32[]{:S(2)}) async-start(), calls=%async_computation.19 | async-start | bytes 1253376 | tf_op jit(solution)/shard_map/reduce_scatter | solution.py:329
  582.5 480.7 %reduce-scatter.20.cloned.1.call-start = ((), (), s32[]{:S(2)}) async-start(), calls=%async_computation.21 | async-start | bytes 5013504 | tf_op jit(solution)/shard_map/reduce_scatter | solution.py:331
  588.9 616.1 %reduce-scatter.18.cloned.1.call-start = ((), (), s32[]{:S(2)}) async-start(), calls=%async_computation.20 | async-start | bytes 5013504 | tf_op jit(solution)/shard_map/reduce_scatter | solution.py:330
  606.8 38.3 %all-to-all-start.1 = ((bf16[16,2,12288]{2,1,0:T(2,128)(2,1)}), bf16[16,2,12288]{2,1,0:T(2,128)(2,1)S(1)}, u32[]{:S(2)}, u32[]{:S(2)}) async-start(bf16[16,2,12288]{2,1,0:T(2,128)(2,1)} %reshape.397), calls=%async_computation.3 | async-start | bytes 1572864 | tf_op jit(solution)/shard_map/all_to_all | solution.py:364
  621.6 33.1 %copy-start.40 = (u32[32]{0:T(128)S(1)}, u32[32]{0:T(128)}, u32[]{:S(2)}) copy-start(u32[32]{0:T(128)} %constant.142) | copy-start | bytes 388
  621.7 34.3 %copy-start.7 = (bf16[1,32,16,768]{3,1,0,2:T(8,128)(2,1)S(1)}, bf16[1,32,16,768]{3,1,0,2:T(8,128)(2,1)}, u32[]{:S(2)}) copy-start(bf16[1,32,16,768]{3,1,0,2:T(8,128)(2,1)} %copy-done.5) | copy-start | bytes 2359300
  622.8 33.4 %copy-start.26 = (f32[768]{0:T(1024)S(1)}, f32[768]{0:T(1024)}, u32[]{:S(2)}) copy-start(f32[768]{0:T(1024)} %get-tuple-element.255) | copy-start | bytes 9220
  645.1 148.2 %all-to-all-start.3 = ((bf16[16,2,12288]{2,1,0:T(2,128)(2,1)}), bf16[16,2,12288]{2,1,0:T(2,128)(2,1)S(1)}, u32[]{:S(2)}, u32[]{:S(2)}) async-start(bf16[16,2,12288]{2,1,0:T(2,128)(2,1)} %reshape.399), calls=%async_computation.7 | async-start | bytes 1572864 | tf_op jit(solution)/shard_map/all_to_all | solution.py:365
  (35 other events, 106.2 us)
Sparse Core Ops, SparseCore 0:
  42.3 7.5 all-gather.11
  52.6 60.9 all-gather.19
  146.1 7.8 reduce-scatter.7
  157.0 63.4 all-gather.21
  222.6 8.6 all-gather.13
  234.3 63.4 all-gather.23
  304.4 7.8 reduce-scatter.9
  338.1 7.5 all-gather.15
  359.0 10.2 reduce-scatter.11
  376.3 10.9 all-gather.17
  569.6 10.1 reduce-scatter.13
  585.4 206.0 all-reduce.4
  797.6 122.5 reduce-scatter.15
  926.6 136.5 reduce-scatter.19
  1068.8 136.2 reduce-scatter.17
